TPU v7x, 128 devices: a whole 4x4x4 slice. The times are simulated.
128 devices in a mesh: grp: 2 (over core), row: 8 (over z, y_lo), col: 8 (over x, y_hi).
Axes of the slice: x: 4, y: 4 (y_hi: 2, y_lo: 2; y = y_hi * 2 + y_lo), z: 4, core: 2. Of those that a mesh axis runs over, the one named last changes fastest.
Arguments:
- cost_matrix: float32 [2, 8192, 8192], P('grp', 'row', 'col'), may hold values from -0.09375 to 0.09375
- coupling_factors: float32 [2, 8192, 1024], P('grp', ('row', 'col')), may hold values from 0.25 to 4
Outputs:
- updated_factors: float32 [2, 8192, 1024], P('grp', ('row', 'col'))
All inputs are finite; a program needn't handle non-finite values. Where the computation divides by a largest or mean magnitude, that divisor is 1e-20 or more.
Results may differ from a plain program's by a relative error of at most 0.0003.
Values sent between devices are 32-bit elements; how exact they have to be, the bound alone decides.
No kernel may reach another device: no remote copies, remote signals or barrier semaphores. Data moves between devices by JAX's collectives and lax.ppermute only.
A program may use at most 64 MiB of HBM per device.

v0:
```python
import jax
import jax.numpy as jnp
from jax import lax
from jax.sharding import PartitionSpec as P

STEPS = 2


def swapped(value, axis, apart):
    return lax.ppermute(value, axis, [(i, i ^ 1 << apart) for i in range(lax.axis_size(axis))])


def shards(cost_matrix, coupling_factors):
    cost_tile = cost_matrix[0]
    current = coupling_factors[0]
    rows_side = lax.axis_size("row")
    blk_rows = cost_tile.shape[0]
    piece_rows = current.shape[0]
    sub_rows = piece_rows // rows_side
    rank_width = current.shape[1]
    for iteration in range(STEPS):
        pieces = current.reshape(rows_side, 1, sub_rows, rank_width)
        turned = lax.all_to_all(
            lax.all_to_all(pieces, "row", split_axis=0, concat_axis=1, tiled=True),
            "col",
            split_axis=1,
            concat_axis=0,
            tiled=True,
        )
        panel_rows = lax.all_gather(turned, "row", axis=1, tiled=True).reshape(blk_rows, rank_width)
        mixed = lax.psum_scatter(
            jnp.dot(
                cost_tile,
                panel_rows,
                precision=lax.Precision.HIGHEST,
                preferred_element_type=jnp.float32,
            ),
            "col",
            scatter_dimension=0,
            tiled=True,
        )
        core_part = lax.dot_general(
            current,
            mixed,
            (((0,), (0,)), ((), ())),
            precision=lax.Precision.HIGHEST,
            preferred_element_type=jnp.float32,
        )
        whole_core = lax.psum(core_part, ("row", "col"))
        other_core = swapped(whole_core, "grp", 0)
        gradient = jnp.dot(
            mixed, other_core, precision=lax.Precision.HIGHEST, preferred_element_type=jnp.float32
        )
        row_scale = jnp.max(jnp.abs(gradient), axis=1, keepdims=True) + 1e-06
        exponent = -3.0 * gradient / row_scale
        weighted = current * jnp.exp(exponent)
        current = rank_width * weighted / jnp.sum(weighted, axis=1, keepdims=True)
    return current[None]


def solution(mesh):
    in_specs = (P("grp", "row", "col"), P("grp", ("row", "col"), None))
    out_specs = P("grp", ("row", "col"), None)
    return jax.shard_map(shards, mesh=mesh, in_specs=in_specs, out_specs=out_specs, check_vma=False)
```

profile of v0, /device:TPU:0, one launch (start us, length us, event | category | flops | bytes accessed | tf_op | source)
XLA Modules:
  0.0 778.7 jit_solution(8991404935783261665)
XLA Ops:
  6.5 16.6 %all_to_all.48 = f32[8,1,16,1024]{3,2,1,0:T(8,128)S(1)} all-to-all(f32[8,1,16,1024]{3,2,1,0:T(8,128)} %bitcast.40), channel_id=1, replica_groups=mesh['grp'=2,'row'=8,'col'=8] {'row'}, dimensions={0} | all-to-all | bytes 1048576 | tf_op jit(solution)/shard_map/all_to_all | solution.py:24
  23.1 16.7 %all_to_all.49 = f32[1,8,16,1024]{3,2,0,1:T(8,128)} all-to-all(f32[1,8,16,1024]{3,2,0,1:T(8,128)S(1)} %bitcast.41), channel_id=1, replica_groups=mesh['grp'=2,'row'=8,'col'=8] {'col'}, dimensions={1} | all-to-all | bytes 1048576 | tf_op jit(solution)/shard_map/all_to_all | solution.py:23
  39.8 0.0 reduce-scatter.3.cloned.1.call-start
  39.9 86.4 %all-gather.5.cloned.1.call-done = f32[1,8,128,1024]{3,2,0,1:T(8,128)} async-done(((f32[1,8,16,1024]{3,2,0,1:T(8,128)}), f32[1,8,128,1024]{3,2,0,1:T(8,128)}) %all-gather.5.cloned.1.call-update) | async-done | bytes 4194320 | tf_op jit(solution)/shard_map/all_gather | solution.py:30
  126.3 17.6 %fusion.2 = f32[1024,1024]{1,0:T(8,128)} fusion(f32[1024,1024]{1,0:T(8,128)} %bitcast.43, f32[1,1024,1024]{2,1,0:T(8,128)} %param.2), kind=kOutput, calls=%fused_computation.2 | convolution fusion | flops 12884901888 | bytes 12582912 | tf_op jit(solution)/shard_map/dot_general | solution.py:32
  143.9 0.0 all-reduce.3.cloned.1.call-start
  143.9 85.1 %reduce-scatter.3.cloned.1.call-done = f32[128,1024]{1,0:T(8,128)} async-done(((f32[1024,1024]{1,0:T(8,128)}), f32[128,1024]{1,0:T(8,128)}) %reduce-scatter.3.cloned.1.call-update) | async-done | bytes 524304 | tf_op jit(solution)/shard_map/reduce_scatter | solution.py:31
  229.0 6.2 convolution_bitcast_fusion
  235.3 137.9 %all-reduce.3.cloned.1.call-done = f32[1024,1024]{0,1:T(8,128)} async-done(((f32[1024,1024]{0,1:T(8,128)}), f32[1024,1024]{0,1:T(8,128)}) %all-reduce.3.cloned.1.call-update) | async-done | bytes 4194320 | tf_op jit(solution)/shard_map/psum | solution.py:49
  373.2 7.4 collective-permute-done
  380.5 4.6 abs_reduce_fusion.1
  385.1 0.3 fusion.9
  385.4 0.1 multiply_divide_fusion
  385.5 13.1 %all_to_all.50 = f32[8,1,16,1024]{3,2,1,0:T(8,128)S(1)} all-to-all(f32[8,1,16,1024]{3,2,1,0:T(8,128)S(1)} %bitcast.39), channel_id=1, replica_groups=mesh['grp'=2,'row'=8,'col'=8] {'row'}, dimensions={0} | all-to-all | bytes 1048576 | tf_op jit(solution)/shard_map/all_to_all | solution.py:24
  398.6 15.2 %all_to_all.51 = f32[1,8,16,1024]{3,2,0,1:T(8,128)} all-to-all(f32[1,8,16,1024]{3,2,0,1:T(8,128)S(1)} %bitcast.42), channel_id=1, replica_groups=mesh['grp'=2,'row'=8,'col'=8] {'col'}, dimensions={1} | all-to-all | bytes 1048576 | tf_op jit(solution)/shard_map/all_to_all | solution.py:23
  413.9 86.7 %all-gather.7.cloned.1.call-done = f32[1,8,128,1024]{3,2,0,1:T(8,128)} async-done(((f32[1,8,16,1024]{3,2,0,1:T(8,128)}), f32[1,8,128,1024]{3,2,0,1:T(8,128)}) %all-gather.7.cloned.1.call-update) | async-done | bytes 4194320 | tf_op jit(solution)/shard_map/all_gather | solution.py:30
  500.6 30.5 %fusion.4 = f32[1024,1024]{0,1:T(8,128)} fusion(f32[1024,1024]{1,0:T(8,128)} %bitcast.44, f32[1,1024,1024]{2,1,0:T(8,128)} %param.2), kind=kOutput, calls=%fused_computation.4 | convolution fusion | flops 12884901888 | bytes 12582912 | tf_op jit(solution)/shard_map/dot_general | solution.py:32
  531.2 85.2 %reduce-scatter.5.cloned.1.call-done = f32[128,1024]{0,1:T(8,128)} async-done(((f32[1024,1024]{0,1:T(8,128)}), f32[128,1024]{0,1:T(8,128)}) %reduce-scatter.5.cloned.1.call-update) | async-done | bytes 524304 | tf_op jit(solution)/shard_map/reduce_scatter | solution.py:31
  616.4 6.2 fusion.10
  622.6 138.0 %all-reduce.5.cloned.1.call-done = f32[1024,1024]{1,0:T(8,128)} async-done(((f32[1024,1024]{1,0:T(8,128)}), f32[1024,1024]{1,0:T(8,128)}) %all-reduce.5.cloned.1.call-update) | async-done | bytes 4194320 | tf_op jit(solution)/shard_map/psum | solution.py:49
  760.6 7.4 collective-permute-done.1
  768.0 2.6 abs_reduce_fusion
  770.6 0.3 fusion.8
  770.9 0.9 divide_bitcast_fusion
  (20 shorter events, 0.3 us)
Async XLA Ops:
  6.5 119.7 %all-gather.5.cloned.1.call-start = ((), (), s32[]{:S(2)}) async-start(), calls=%async_computation.10 | async-start | bytes 4718592 | tf_op jit(solution)/shard_map/all_gather | solution.py:30
  39.8 189.1 %reduce-scatter.3.cloned.1.call-start = ((), (), s32[]{:S(2)}) async-start(), calls=%async_computation.6 | async-start | bytes 4718592 | tf_op jit(solution)/shard_map/reduce_scatter | solution.py:31
  143.8 85.2 %copy-start = (f32[1,128,1024]{2,1,0:T(8,128)S(1)}, f32[1,128,1024]{2,1,0:T(8,128)}, u32[]{:S(2)}) copy-start(f32[1,128,1024]{2,1,0:T(8,128)} %param.3) | copy-start | bytes 1572868
  143.9 229.3 %all-reduce.3.cloned.1.call-start = ((), (), s32[]{:S(2)}) async-start(), calls=%async_computation.7 | async-start | bytes 8388608 | tf_op jit(solution)/shard_map/psum | solution.py:49
  229.0 151.6 %copy-start.1 = (f32[128,1024]{1,0:T(8,128)S(1)}, f32[128,1024]{1,0:T(8,128)}, u32[]{:S(2)}) copy-start(f32[128,1024]{1,0:T(8,128)} %reduce-scatter.3.cloned.1.call-done) | copy-start | bytes 1572868
  235.2 265.4 %all-gather.7.cloned.1.call-start = ((), (), s32[]{:S(2)}) async-start(), calls=%async_computation.11 | async-start | bytes 4718592 | tf_op jit(solution)/shard_map/all_gather | solution.py:30
  373.2 7.4 collective-permute-start
  413.8 202.5 %reduce-scatter.5.cloned.1.call-start = ((), (), s32[]{:S(2)}) async-start(), calls=%async_computation.8 | async-start | bytes 4718592 | tf_op jit(solution)/shard_map/reduce_scatter | solution.py:31
  531.1 229.5 %all-reduce.5.cloned.1.call-start = ((), (), s32[]{:S(2)}) async-start(), calls=%async_computation.9 | async-start | bytes 8388608 | tf_op jit(solution)/shard_map/psum | solution.py:49
  616.4 151.6 %copy-start.2 = (f32[128,1024]{0,1:T(8,128)S(1)}, f32[128,1024]{0,1:T(8,128)}, u32[]{:S(2)}) copy-start(f32[128,1024]{0,1:T(8,128)} %reduce-scatter.5.cloned.1.call-done) | copy-start | bytes 1572868
  760.6 7.4 collective-permute-start.1
Sparse Core Ops, SparseCore 0:
  40.0 86.2 all-gather.4
  144.0 84.9 reduce-scatter.2
  235.3 137.7 all-reduce.2
  413.9 86.6 all-gather.6
  531.2 85.0 reduce-scatter.4
  622.7 137.8 all-reduce.4
where the time goes:
time: 780 us; the launch traced here: 779 us
  waiting for transfers between devices  634 us (81%)
  matrix products  67.6 us (9%)
  blocking collectives  61.6 us (8%)
  between operations  13.5 us (2%)
    psum x2, waiting for transfers between devices, shards(): whole_core = lax.psum(core_part, ('row', 'col'))  276 us
    all_gather x2, waiting for transfers between devices, shards(): lax.all_gather(turned, 'row', axis=1, tiled=True)  173 us
    reduce_scatter x2, waiting for transfers between devices, shards(): lax.psum_scatter(jnp.dot(cost_tile, panel_rows, precision=lax.Precision.H...  170 us
    dot_general x2, matrix products, shards(): jnp.dot(cost_tile, panel_rows, precision=lax.Precision.HIGHEST, preferred...  48.1 us
    all_to_all x2, blocking collectives, shards(): lax.all_to_all(lax.all_to_all(pieces, 'row', split_axis=0, concat_axis=1,...  31.9 us
    all_to_all x2, blocking collectives, shards(): lax.all_to_all(pieces, 'row', split_axis=0, concat_axis=1, tiled=True)  29.7 us
  transfers between devices with their start and end apart: 8, of which 8 were waited for; matrix products, arithmetic and copies ran while one was open for 0% of the time, Pallas kernels for 0%

commit v1 on v0

v1 whole, which is shorter than its diff:
```python
import jax
import jax.numpy as jnp
from jax import lax
from jax.sharding import PartitionSpec as P

STEPS = 2
HIGH = lax.Precision.HIGH


def exchange(pieces, axes):
    return lax.all_to_all(pieces, axes, split_axis=0, concat_axis=0, tiled=True)


def dot(a, b, contract):
    return lax.dot_general(
        a, b, (contract, ((), ())), precision=HIGH, preferred_element_type=jnp.float32
    )


def shards(cost_matrix, coupling_factors):
    cost_tile = cost_matrix[0]
    current = coupling_factors[0]
    rows_side = lax.axis_size("row")
    cols_side = lax.axis_size("col")
    everyone = rows_side * cols_side
    blk_rows = cost_tile.shape[0]
    piece_rows, rank_width = current.shape
    sub_rows = piece_rows // rows_side
    core_rows = rank_width // everyone
    swap = [(i, i ^ 1) for i in range(lax.axis_size("grp"))]
    current = exchange(current, "row")
    for iteration in range(STEPS):
        pieces = current.reshape(cols_side, 1, sub_rows, rank_width)
        sent = jnp.broadcast_to(pieces, (cols_side, rows_side, sub_rows, rank_width))
        panel_rows = exchange(
            sent.reshape(everyone * sub_rows, rank_width), ("col", "row")
        )
        partial = dot(cost_tile, panel_rows, ((1,), (0,)))
        parts = exchange(partial, ("col", "row"))
        mixed = parts.reshape(cols_side, piece_rows, rank_width).sum(0)
        core_part = dot(current, mixed, ((0,), (0,)))
        core_rows_parts = exchange(core_part, ("row", "col"))
        core_piece = core_rows_parts.reshape(everyone, core_rows, rank_width).sum(0)
        other_piece = lax.ppermute(core_piece, "grp", swap)
        other_core = exchange(
            jnp.broadcast_to(other_piece[None], (everyone, core_rows, rank_width)).reshape(
                rank_width, rank_width
            ),
            ("row", "col"),
        )
        gradient = dot(mixed, other_core, ((1,), (0,)))
        row_scale = jnp.max(jnp.abs(gradient), axis=1, keepdims=True) + 1e-06
        exponent = -3.0 * gradient / row_scale
        weighted = current * jnp.exp(exponent)
        current = rank_width * weighted / jnp.sum(weighted, axis=1, keepdims=True)
    return exchange(current, "row")[None]


def solution(mesh):
    in_specs = (P("grp", "row", "col"), P("grp", ("row", "col"), None))
    out_specs = P("grp", ("row", "col"), None)
    return jax.shard_map(shards, mesh=mesh, in_specs=in_specs, out_specs=out_specs, check_vma=False)
```

time: 780 us -> 542 us (0.69)
  waiting for transfers between devices: 634 us -> 54.6 us
  blocking collectives: 61.6 us -> 444 us
  matrix products: 67.6 us -> 22.1 us
  between operations: 13.5 us -> 0.15 us
  starting transfers between devices: 0.22 us -> 8.39 us
    all_to_all x4 -> x9, blocking collectives: 61.6 us -> 444 us  [exchange(): return lax.all_to_all(pieces, axes, split_axis=0, concat_axis=0, tiled=True)]
    psum x2 -> x0, waiting for transfers between devices: 276 us -> none  [shards(): whole_core = lax.psum(core_part, ('row', 'col'))]
    all_gather x2 -> x0, waiting for transfers between devices: 173 us -> none  [shards(): lax.all_gather(turned, 'row', axis=1, tiled=True)]
    reduce_scatter x2 -> x0, waiting for transfers between devices: 170 us -> none  [shards(): lax.psum_scatter(jnp.dot(cost_tile, panel_rows, precision=lax.Precision.H...]
    all_to_all x0 -> x1, waiting for transfers between devices: none -> 52.1 us  [exchange(): return lax.all_to_all(pieces, axes, split_axis=0, concat_axis=0, tiled=True)]
    dot_general x6, matrix products: 67.6 us -> 22.1 us  [dot(): lax.dot_general(a, b, (contract, ((), ())), precision=HIGH, preferred_ele...]
    ppermute x2, waiting for transfers between devices: 14.7 us -> 2.48 us  [shards(): other_piece = lax.ppermute(core_piece, 'grp', swap)]
    all_to_all x0 -> x1, starting transfers between devices: none -> 8.22 us  [exchange(): return lax.all_to_all(pieces, axes, split_axis=0, concat_axis=0, tiled=True)]
  transfers between devices with their start and end apart: 8 -> 3, of which waited for: 8 -> 3; matrix products, arithmetic and copies ran while one was open for 0% -> 0% of each run, Pallas kernels for 0% -> 0%
where the time goes in v1:
time: 542 us; the launch traced here: 541 us
  blocking collectives  444 us (82%)
  waiting for transfers between devices  54.6 us (10%)
  matrix products  22.1 us (4%)
  other arithmetic  8.76 us (2%)
  starting transfers between devices  8.39 us (2%)
    all_to_all x9, blocking collectives, exchange(): return lax.all_to_all(pieces, axes, split_axis=0, concat_axis=0, tiled=True)  444 us
    all_to_all x1, waiting for transfers between devices, exchange(): return lax.all_to_all(pieces, axes, split_axis=0, concat_axis=0, tiled=True)  52.1 us
    dot_general x6, matrix products, dot(): lax.dot_general(a, b, (contract, ((), ())), precision=HIGH, preferred_ele...  22.1 us
  transfers between devices with their start and end apart: 3, of which 3 were waited for; matrix products, arithmetic and copies ran while one was open for 0% of the time, Pallas kernels for 0%

profile of v1, /device:TPU:0, one launch (start us, length us, event | category | flops | bytes accessed | tf_op | source)
XLA Modules:
  0.0 541.3 jit_solution(16276561162254469941)
XLA Ops:
  0.0 16.6 %all_to_all.93 = f32[8,16,1024]{2,1,0:T(8,128)S(1)} all-to-all(f32[8,16,1024]{2,1,0:T(8,128)} %bitcast.61), channel_id=1, replica_groups=mesh['grp'=2,'row'=8,'col'=8] {'row'}, dimensions={0} | all-to-all | bytes 1048576 | tf_op jit(solution)/shard_map/all_to_all | solution.py:11
  16.6 0.5 broadcast_in_dim.12
  17.1 59.3 %all_to_all.94 = f32[64,16,1024]{2,1,0:T(8,128)S(1)} all-to-all(f32[64,16,1024]{2,1,0:T(8,128)S(1)} %bitcast.52), channel_id=1, replica_groups=mesh['grp'=2,'row'=8,'col'=8] {'col','row'}, dimensions={0} | all-to-all | bytes 8388608 | tf_op jit(solution)/shard_map/all_to_all | solution.py:11
  76.4 6.7 %fusion.6 = f32[64,16,1024]{2,1,0:T(8,128)S(1)} fusion(f32[64,16,1024]{2,1,0:T(8,128)S(1)} %bitcast.62, f32[1024,1024,1]{1,0,2:T(8,128)S(1)} %bitcast.55), kind=kOutput, calls=%fused_computation.16 | convolution fusion | flops 6442450944 | bytes 12582912 | tf_op jit(solution)/shard_map/dot_general | solution.py:15
  83.1 59.9 %all_to_all.95 = f32[64,16,1024]{2,1,0:T(8,128)S(1)} all-to-all(f32[64,16,1024]{2,1,0:T(8,128)S(1)} %fusion.6), channel_id=1, replica_groups=mesh['grp'=2,'row'=8,'col'=8] {'col','row'}, dimensions={0} | all-to-all | bytes 8388608 | tf_op jit(solution)/shard_map/all_to_all | solution.py:11
  143.4 1.8 fusion.7
  145.3 59.6 %all_to_all.96 = f32[64,16,1024]{2,1,0:T(8,128)} all-to-all(f32[64,16,1024]{2,1,0:T(8,128)S(1)} %bitcast.47), channel_id=1, replica_groups=mesh['grp'=2,'row'=8,'col'=8] {'row','col'}, dimensions={0} | all-to-all | bytes 8388608 | tf_op jit(solution)/shard_map/all_to_all | solution.py:11
  204.9 2.4 reduce_sum.55
  207.4 1.2 collective-permute-done
  209.1 58.6 %all_to_all.97 = f32[64,16,1024]{2,1,0:T(8,128)S(1)} all-to-all(f32[64,16,1024]{2,1,0:T(8,128)S(1)} %broadcast_in_dim.13), channel_id=1, replica_groups=mesh['grp'=2,'row'=8,'col'=8] {'row','col'}, dimensions={0} | all-to-all | bytes 8388608 | tf_op jit(solution)/shard_map/all_to_all | solution.py:11
  267.8 1.7 abs_reduce_fusion.1
  270.4 56.5 %all_to_all.98 = f32[64,16,1024]{2,1,0:T(8,128)S(1)} all-to-all(f32[64,16,1024]{2,1,0:T(8,128)S(1)} %bitcast.51), channel_id=1, replica_groups=mesh['grp'=2,'row'=8,'col'=8] {'col','row'}, dimensions={0} | all-to-all | bytes 8388608 | tf_op jit(solution)/shard_map/all_to_all | solution.py:11
  327.0 8.3 %fusion = f32[1024,1024]{0,1:T(8,128)} fusion(f32[1024,1024]{1,0:T(8,128)S(1)} %bitcast.56, f32[1,1024,1024]{2,1,0:T(8,128)S(1)} %copy-done.1), kind=kOutput, calls=%fused_computation.1 | convolution fusion | flops 6442450944 | bytes 12582912 | tf_op jit(solution)/shard_map/dot_general | solution.py:15
  335.3 8.2 %all-to-all-start.6 = ((f32[64,16,1024]{2,1,0:T(8,128)}), f32[64,16,1024]{2,1,0:T(8,128)}, u32[]{:S(2)}, u32[]{:S(2)}) async-start(f32[64,16,1024]{2,1,0:T(8,128)} %bitcast.54), calls=%async_computation.6 | async-start | bytes 8388608 | tf_op jit(solution)/shard_map/all_to_all | solution.py:11
  343.8 52.1 %all-to-all-done.6 = f32[64,16,1024]{2,1,0:T(8,128)} async-done(((f32[64,16,1024]{2,1,0:T(8,128)}), f32[64,16,1024]{2,1,0:T(8,128)}, u32[]{:S(2)}, u32[]{:S(2)}) %all-to-all-start.6) | async-done | bytes 4194336 | tf_op jit(solution)/shard_map/all_to_all | solution.py:11
  395.9 2.6 bitcast_reduce_fusion
  398.5 1.8 fusion.2
  400.3 63.9 %all_to_all.99 = f32[64,16,1024]{2,1,0:T(8,128)} all-to-all(f32[64,16,1024]{2,1,0:T(8,128)S(1)} %fusion.2), channel_id=1, replica_groups=mesh['grp'=2,'row'=8,'col'=8] {'row','col'}, dimensions={0} | all-to-all | bytes 8388608 | tf_op jit(solution)/shard_map/all_to_all | solution.py:11
  464.2 2.4 reduce_sum.58
  466.7 1.2 collective-permute-done.1
  468.5 57.6 %all_to_all.100 = f32[64,16,1024]{2,1,0:T(8,128)S(1)} all-to-all(f32[64,16,1024]{2,1,0:T(8,128)S(1)} %broadcast_in_dim.16), channel_id=1, replica_groups=mesh['grp'=2,'row'=8,'col'=8] {'row','col'}, dimensions={0} | all-to-all | bytes 8388608 | tf_op jit(solution)/shard_map/all_to_all | solution.py:11
  526.1 1.7 abs_reduce_fusion
  528.3 12.2 %all_to_all.101 = f32[8,16,1024]{2,1,0:T(8,128)S(1)} all-to-all(f32[8,16,1024]{2,1,0:T(8,128)S(1)} %bitcast.59), channel_id=1, replica_groups=mesh['grp'=2,'row'=8,'col'=8] {'row'}, dimensions={0} | all-to-all | bytes 1048576 | tf_op jit(solution)/shard_map/all_to_all | solution.py:11
  540.5 0.8 copy.6
  (18 shorter events, 3.2 us)
Async XLA Ops:
  17.1 59.3 %copy-start = (f32[1,1024,1024]{2,1,0:T(8,128)S(1)}, f32[1,1024,1024]{2,1,0:T(8,128)}, u32[]{:S(2)}) copy-start(f32[1,1024,1024]{2,1,0:T(8,128)} %param.2) | copy-start | bytes 12582916
  207.3 1.3 collective-permute-start
  270.4 56.5 %copy-start.1 = (f32[1,1024,1024]{2,1,0:T(8,128)S(1)}, f32[1,1024,1024]{2,1,0:T(8,128)}, u32[]{:S(2)}) copy-start(f32[1,1024,1024]{2,1,0:T(8,128)} %param.2) | copy-start | bytes 12582916
  335.3 60.7 %all-to-all-start.6 = ((f32[64,16,1024]{2,1,0:T(8,128)}), f32[64,16,1024]{2,1,0:T(8,128)}, u32[]{:S(2)}, u32[]{:S(2)}) async-start(f32[64,16,1024]{2,1,0:T(8,128)} %bitcast.54), calls=%async_computation.6 | async-start | bytes 8388608 | tf_op jit(solution)/shard_map/all_to_all | solution.py:11
  466.6 1.3 collective-permute-start.1

commit v2 on v1

v2 whole, which is shorter than its diff:
```python
import jax
import jax.numpy as jnp
from jax import lax
from jax.sharding import Mesh
from jax.sharding import PartitionSpec as P

STEPS = 2
HIGH = lax.Precision.HIGH
SIZES = {"grp": 2, "z": 4, "yl": 2, "x": 4, "yh": 2}
PLANE = ("x", "yh", "yl")


def exchange(pieces, axes):
    return lax.all_to_all(pieces, axes, split_axis=0, concat_axis=0, tiled=True)


def spread(piece, axes, count):
    return exchange(jnp.broadcast_to(piece[None], (count,) + piece.shape), axes)


def dot(a, b, contract):
    return lax.dot_general(
        a, b, (contract, ((), ())), precision=HIGH, preferred_element_type=jnp.float32
    )


def shards(cost_matrix, coupling_factors):
    nz, nyl, nx, nyh = (SIZES[a] for a in ("z", "yl", "x", "yh"))
    blocks, plane = nz * nyl, nx * nyh * nyl
    cost_tile = cost_matrix[0]
    start = coupling_factors[0]
    blk_rows = cost_tile.shape[0]
    piece_rows, rank = start.shape
    sub, wide = piece_rows // nyl, rank // nz
    rows = blocks * sub
    swap = [(0, 1), (1, 0)]
    start = start.reshape(nyl, sub, nz, wide).transpose(2, 0, 1, 3)
    current = exchange(start.reshape(blocks, sub, wide), ("z", "yl"))
    for iteration in range(STEPS):
        flat = current.reshape(rows, wide)
        whole = spread(flat, "z", nz)
        sent = jnp.broadcast_to(current[:, None], (blocks, nyl, sub, wide))
        panel = exchange(sent.reshape(plane, sub, wide), PLANE).reshape(blk_rows, wide)
        panels = spread(panel, "z", nz)
        partial = jnp.einsum(
            "mk,zkn->mzn", cost_tile, panels, precision=HIGH, preferred_element_type=jnp.float32
        ).reshape(nx, blk_rows // nx, rank)
        half = exchange(partial, "x").sum(0)
        half = half.reshape(nyh, nyl, sub, nz, wide).transpose(0, 3, 1, 2, 4)
        mixed = exchange(half.reshape(nyh * blocks, sub, wide), ("yh", "z", "yl"))
        mixed = mixed.reshape(nyh, rows, wide).sum(0)
        mixed_whole = spread(mixed, "z", nz)
        core_part = jnp.einsum(
            "zra,rn->zan", whole, mixed, precision=HIGH, preferred_element_type=jnp.float32
        )
        core = exchange(core_part.reshape(plane, rank // plane, wide), PLANE).sum(0)
        core = lax.ppermute(core, "grp", swap)
        core = spread(core, PLANE, plane).reshape(nz, wide, wide)
        gradient = jnp.einsum(
            "zra,zan->rn", mixed_whole, core, precision=HIGH, preferred_element_type=jnp.float32
        )
        top = spread(jnp.max(jnp.abs(gradient), axis=1), "z", nz).max(0)
        row_scale = top[:, None] + 1e-06
        weighted = flat * jnp.exp(-3.0 * gradient / row_scale)
        total = spread(jnp.sum(weighted, axis=1), "z", nz).sum(0)
        current = (rank * weighted / total[:, None]).reshape(blocks, sub, wide)
    out = exchange(current, ("z", "yl")).reshape(nz, nyl, sub, wide)
    return out.transpose(1, 2, 0, 3).reshape(1, piece_rows, rank)


def solution(mesh):
    fine = Mesh(mesh.devices.reshape(tuple(SIZES.values())), tuple(SIZES))
    in_specs = (P("grp", ("z", "yl"), ("x", "yh")), P("grp", ("z", "yl", "x", "yh"), None))
    out_specs = P("grp", ("z", "yl", "x", "yh"), None)
    return jax.shard_map(shards, mesh=fine, in_specs=in_specs, out_specs=out_specs, check_vma=False)
```

time: 542 us -> 518 us (0.956)
  blocking collectives: 444 us -> 340 us
  waiting for transfers between devices: 54.6 us -> 97.2 us
  local copies, waits for them, and re-layouts: 3.05 us -> 24 us
  starting transfers between devices: 8.39 us -> 21.9 us
    all_to_all x9 -> x16, blocking collectives: 444 us -> 340 us  [exchange(): return lax.all_to_all(pieces, axes, split_axis=0, concat_axis=0, tiled=True)]
    all_to_all x1 -> x6, waiting for transfers between devices: 52.1 us -> 94.8 us  [exchange(): return lax.all_to_all(pieces, axes, split_axis=0, concat_axis=0, tiled=True)]
    all_to_all x1 -> x6, starting transfers between devices: 8.22 us -> 21.7 us  [exchange(): return lax.all_to_all(pieces, axes, split_axis=0, concat_axis=0, tiled=True)]
    reshape x0 -> x7, local copies, waits for them, and re-layouts: none -> 11.2 us  [the longest x2 8.61 us: shards(): partial = jnp.einsum('mk,zkn->mzn', cost_tile, panels, precision=HIGH, pr...]
    broadcast_in_dim x4 -> x16, local copies, waits for them, and re-layouts: 2.05 us -> 8.49 us  [the longest x14 8.29 us: spread(): return exchange(jnp.broadcast_to(piece[None], (count,) + piece.shape), axes)]
    reduce_sum x6 -> x10, other arithmetic: 8.41 us -> 12.3 us  [the longest x2 5.31 us: shards(): half = exchange(partial, 'x').sum(0)]
  transfers between devices with their start and end apart: 3 -> 8, of which waited for: 3 -> 8; matrix products, arithmetic and copies ran while one was open for 0% -> 1% of each run, Pallas kernels for 0% -> 0%
where the time goes in v2:
time: 518 us; the launch traced here: 516 us
  blocking collectives  340 us (66%)
  waiting for transfers between devices  97.2 us (19%)
  local copies, waits for them, and re-layouts  24 us (5%)
  starting transfers between devices  21.9 us (4%)
  matrix products  20 us (4%)
  other arithmetic  12.6 us (2%)
    all_to_all x16, blocking collectives, exchange(): return lax.all_to_all(pieces, axes, split_axis=0, concat_axis=0, tiled=True)  340 us
    all_to_all x6, waiting for transfers between devices, exchange(): return lax.all_to_all(pieces, axes, split_axis=0, concat_axis=0, tiled=True)  94.8 us
    all_to_all x6, starting transfers between devices, exchange(): return lax.all_to_all(pieces, axes, split_axis=0, concat_axis=0, tiled=True)  21.7 us
    dot_general x2, matrix products, shards(): jnp.einsum('mk,zkn->mzn', cost_tile, panels, precision=HIGH, preferred_el...  15 us
  transfers between devices with their start and end apart: 8, of which 8 were waited for; matrix products, arithmetic and copies ran while one was open for 1% of the time, Pallas kernels for 0%

profile of v2, /device:TPU:0, one launch (start us, length us, event | category | flops | bytes accessed | tf_op | source)
XLA Modules:
  0.0 516.0 jit_solution(10865285518771946494)
XLA Ops:
  1.4 16.4 %all_to_all.114 = f32[8,64,256]{2,1,0:T(8,128)S(1)} all-to-all(f32[8,64,256]{2,1,0:T(8,128)S(1)} %bitcast.84), channel_id=1, replica_groups=mesh['grp'=2,'z'=4,'yl'=2,'x'=4,'yh'=2] {'z','yl'}, dimensions={0} | all-to-all | bytes 1048576 | tf_op jit(solution)/shard_map/all_to_all | solution.py:14
  17.9 22.5 %all_to_all.115 = f32[16,64,256]{2,1,0:T(8,128)S(1)} all-to-all(f32[16,64,256]{2,1,0:T(8,128)S(1)} %bitcast.81), channel_id=1, replica_groups=mesh['grp'=2,'z'=4,'yl'=2,'x'=4,'yh'=2] {'x','yh','yl'}, dimensions={0} | all-to-all | bytes 2097152 | tf_op jit(solution)/shard_map/all_to_all | solution.py:14
  41.2 49.5 %all_to_all.116 = f32[4,1024,256]{1,2,0:T(8,128)S(1)} all-to-all(f32[4,1024,256]{1,2,0:T(8,128)S(1)} %broadcast_in_dim.36), channel_id=1, replica_groups=mesh['grp'=2,'z'=4,'yl'=2,'x'=4,'yh'=2] {'z'}, dimensions={0} | all-to-all | bytes 8388608 | tf_op jit(solution)/shard_map/all_to_all | solution.py:14
  90.8 6.7 %fusion.11 = f32[4,256,1024]{2,1,0:T(8,128)S(1)} fusion(f32[4,256,1024]{2,1,0:T(8,128)S(1)} %bitcast.88, f32[1024,1024,1]{1,0,2:T(8,128)S(1)} %bitcast.74), kind=kOutput, calls=%fused_computation.22 | convolution fusion | flops 6442450944 | bytes 12582912 | tf_op jit(solution)/shard_map/mk,zkn->mzn/dot_general | solution.py:45
  97.5 49.3 %all_to_all.117 = f32[4,256,1024]{2,1,0:T(8,128)} all-to-all(f32[4,256,1024]{2,1,0:T(8,128)S(1)} %fusion.11), channel_id=1, replica_groups=mesh['grp'=2,'z'=4,'yl'=2,'x'=4,'yh'=2] {'x'}, dimensions={0} | all-to-all | bytes 8388608 | tf_op jit(solution)/shard_map/all_to_all | solution.py:14
  155.1 13.7 %all-to-all-done.4 = f32[16,64,256]{2,1,0:T(8,128)S(1)} async-done(((f32[16,64,256]{2,1,0:T(8,128)}), f32[16,64,256]{2,1,0:T(8,128)S(1)}, u32[]{:S(2)}, u32[]{:S(2)}) %all-to-all-start.4) | async-done | bytes 1048608 | tf_op jit(solution)/shard_map/all_to_all | solution.py:14
  175.4 20.7 %all-to-all-done.6 = f32[4,512,256]{1,2,0:T(8,128)S(1)} async-done(((f32[4,512,256]{1,2,0:T(8,128)}), f32[4,512,256]{1,2,0:T(8,128)S(1)}, u32[]{:S(2)}, u32[]{:S(2)}) %all-to-all-start.6) | async-done | bytes 2097184 | tf_op jit(solution)/shard_map/all_to_all | solution.py:14
  197.1 16.2 %all_to_all.118 = f32[16,64,256]{2,1,0:T(8,128)} all-to-all(f32[16,64,256]{2,1,0:T(8,128)S(1)} %bitcast.73), channel_id=1, replica_groups=mesh['grp'=2,'z'=4,'yl'=2,'x'=4,'yh'=2] {'x','yh','yl'}, dimensions={0} | all-to-all | bytes 2097152 | tf_op jit(solution)/shard_map/all_to_all | solution.py:14
  221.1 18.3 %all-to-all-done.5 = f32[4,512,256]{2,1,0:T(8,128)S(1)} async-done(((f32[4,512,256]{2,1,0:T(8,128)}), f32[4,512,256]{2,1,0:T(8,128)S(1)}, u32[]{:S(2)}, u32[]{:S(2)}) %all-to-all-start.5) | async-done | bytes 2097184 | tf_op jit(solution)/shard_map/all_to_all | solution.py:14
  239.5 16.2 %all_to_all.119 = f32[16,64,256]{2,1,0:T(8,128)S(1)} all-to-all(f32[16,64,256]{2,1,0:T(8,128)S(1)} %broadcast_in_dim.39), channel_id=1, replica_groups=mesh['grp'=2,'z'=4,'yl'=2,'x'=4,'yh'=2] {'x','yh','yl'}, dimensions={0} | all-to-all | bytes 2097152 | tf_op jit(solution)/shard_map/all_to_all | solution.py:14
  257.5 7.6 %all_to_all.120 = f32[4,1,512]{2,1,0:T(1,128)S(1)} all-to-all(f32[4,1,512]{2,1,0:T(1,128)S(1)} %broadcast_in_dim.40), channel_id=1, replica_groups=mesh['grp'=2,'z'=4,'yl'=2,'x'=4,'yh'=2] {'z'}, dimensions={0} | all-to-all | bytes 16384 | tf_op jit(solution)/shard_map/all_to_all | solution.py:14
  266.5 7.7 %all_to_all.121 = f32[4,1,512]{2,1,0:T(1,128)S(1)} all-to-all(f32[4,1,512]{2,1,0:T(1,128)S(1)} %broadcast_in_dim.41), channel_id=1, replica_groups=mesh['grp'=2,'z'=4,'yl'=2,'x'=4,'yh'=2] {'z'}, dimensions={0} | all-to-all | bytes 16384 | tf_op jit(solution)/shard_map/all_to_all | solution.py:14
  274.5 16.2 %all_to_all.122 = f32[16,64,256]{2,1,0:T(8,128)S(1)} all-to-all(f32[16,64,256]{2,1,0:T(8,128)S(1)} %bitcast.82), channel_id=1, replica_groups=mesh['grp'=2,'z'=4,'yl'=2,'x'=4,'yh'=2] {'x','yh','yl'}, dimensions={0} | all-to-all | bytes 2097152 | tf_op jit(solution)/shard_map/all_to_all | solution.py:14
  291.5 40.0 %all_to_all.123 = f32[4,1024,256]{1,2,0:T(8,128)S(1)} all-to-all(f32[4,1024,256]{1,2,0:T(8,128)S(1)} %broadcast_in_dim.45), channel_id=1, replica_groups=mesh['grp'=2,'z'=4,'yl'=2,'x'=4,'yh'=2] {'z'}, dimensions={0} | all-to-all | bytes 8388608 | tf_op jit(solution)/shard_map/all_to_all | solution.py:14
  331.5 8.3 %fusion.2 = f32[1024,4,256]{0,2,1:T(8,128)} fusion(f32[4,1024,256]{1,2,0:T(8,128)S(1)} %all_to_all.123, f32[1,1024,1024]{2,1,0:T(8,128)S(1)} %copy-done.3), kind=kOutput, calls=%fused_computation.2 | convolution fusion | flops 6442450944 | bytes 12582912 | tf_op jit(solution)/shard_map/mk,zkn->mzn/dot_general | solution.py:45
  348.4 39.4 %all_to_all.124 = f32[4,256,1024]{1,2,0:T(8,128)} all-to-all(f32[4,256,1024]{1,2,0:T(8,128)S(1)} %copy.52), channel_id=1, replica_groups=mesh['grp'=2,'z'=4,'yl'=2,'x'=4,'yh'=2] {'x'}, dimensions={0} | all-to-all | bytes 8388608 | tf_op jit(solution)/shard_map/all_to_all | solution.py:14
  396.3 13.1 %all-to-all-done.14 = f32[16,64,256]{2,1,0:T(8,128)S(1)} async-done(((f32[16,64,256]{2,1,0:T(8,128)}), f32[16,64,256]{2,1,0:T(8,128)S(1)}, u32[]{:S(2)}, u32[]{:S(2)}) %all-to-all-start.14) | async-done | bytes 1048608 | tf_op jit(solution)/shard_map/all_to_all | solution.py:14
  416.0 15.1 %all-to-all-done.16 = f32[4,512,256]{1,2,0:T(8,128)S(1)} async-done(((f32[4,512,256]{1,2,0:T(8,128)}), f32[4,512,256]{1,2,0:T(8,128)S(1)}, u32[]{:S(2)}, u32[]{:S(2)}) %all-to-all-start.16) | async-done | bytes 2097184 | tf_op jit(solution)/shard_map/all_to_all | solution.py:14
  432.2 16.4 %all_to_all.125 = f32[16,64,256]{2,1,0:T(8,128)} all-to-all(f32[16,64,256]{2,1,0:T(8,128)S(1)} %fusion.5), channel_id=1, replica_groups=mesh['grp'=2,'z'=4,'yl'=2,'x'=4,'yh'=2] {'x','yh','yl'}, dimensions={0} | all-to-all | bytes 2097152 | tf_op jit(solution)/shard_map/all_to_all | solution.py:14
  456.3 13.8 %all-to-all-done.15 = f32[4,512,256]{2,1,0:T(8,128)S(1)} async-done(((f32[4,512,256]{2,1,0:T(8,128)}), f32[4,512,256]{2,1,0:T(8,128)S(1)}, u32[]{:S(2)}, u32[]{:S(2)}) %all-to-all-start.15) | async-done | bytes 2097184 | tf_op jit(solution)/shard_map/all_to_all | solution.py:14
  470.3 16.2 %all_to_all.126 = f32[16,64,256]{2,1,0:T(8,128)S(1)} all-to-all(f32[16,64,256]{2,1,0:T(8,128)S(1)} %broadcast_in_dim.48), channel_id=1, replica_groups=mesh['grp'=2,'z'=4,'yl'=2,'x'=4,'yh'=2] {'x','yh','yl'}, dimensions={0} | all-to-all | bytes 2097152 | tf_op jit(solution)/shard_map/all_to_all | solution.py:14
  487.6 7.7 %all_to_all.127 = f32[4,1,512]{2,1,0:T(1,128)S(1)} all-to-all(f32[4,1,512]{2,1,0:T(1,128)S(1)} %broadcast_in_dim.49), channel_id=1, replica_groups=mesh['grp'=2,'z'=4,'yl'=2,'x'=4,'yh'=2] {'z'}, dimensions={0} | all-to-all | bytes 16384 | tf_op jit(solution)/shard_map/all_to_all | solution.py:14
  495.6 7.7 %all_to_all.128 = f32[4,1,512]{2,1,0:T(1,128)S(1)} all-to-all(f32[4,1,512]{2,1,0:T(1,128)S(1)} %broadcast_in_dim.50), channel_id=1, replica_groups=mesh['grp'=2,'z'=4,'yl'=2,'x'=4,'yh'=2] {'z'}, dimensions={0} | all-to-all | bytes 16384 | tf_op jit(solution)/shard_map/all_to_all | solution.py:14
  503.5 11.1 %all_to_all.129 = f32[8,64,256]{2,1,0:T(8,128)S(1)} all-to-all(f32[8,64,256]{2,1,0:T(8,128)S(1)} %bitcast.83), channel_id=1, replica_groups=mesh['grp'=2,'z'=4,'yl'=2,'x'=4,'yh'=2] {'z','yl'}, dimensions={0} | all-to-all | bytes 1048576 | tf_op jit(solution)/shard_map/all_to_all | solution.py:14
  (67 shorter events, 66.0 us)
Async XLA Ops:
  41.2 49.6 %copy-start.2 = (f32[1,1024,1024]{2,1,0:T(8,128)S(1)}, f32[1,1024,1024]{2,1,0:T(8,128)}, u32[]{:S(2)}) copy-start(f32[1,1024,1024]{2,1,0:T(8,128)} %param.2) | copy-start | bytes 12582916
  151.2 17.5 %all-to-all-start.4 = ((f32[16,64,256]{2,1,0:T(8,128)}), f32[16,64,256]{2,1,0:T(8,128)S(1)}, u32[]{:S(2)}, u32[]{:S(2)}) async-start(f32[16,64,256]{2,1,0:T(8,128)} %bitcast.10), calls=%async_computation.4 | async-start | bytes 2097152 | tf_op jit(solution)/shard_map/all_to_all | solution.py:14
  168.7 1.7 copy-start.1
  170.4 25.7 %all-to-all-start.6 = ((f32[4,512,256]{1,2,0:T(8,128)}), f32[4,512,256]{1,2,0:T(8,128)S(1)}, u32[]{:S(2)}, u32[]{:S(2)}) async-start(f32[4,512,256]{1,2,0:T(8,128)} %broadcast_in_dim.38), calls=%async_computation.6 | async-start | bytes 4194304 | tf_op jit(solution)/shard_map/all_to_all | solution.py:14
  214.8 24.6 %all-to-all-start.5 = ((f32[4,512,256]{2,1,0:T(8,128)}), f32[4,512,256]{2,1,0:T(8,128)S(1)}, u32[]{:S(2)}, u32[]{:S(2)}) async-start(f32[4,512,256]{2,1,0:T(8,128)} %broadcast_in_dim.37), calls=%async_computation.5 | async-start | bytes 4194304 | tf_op jit(solution)/shard_map/all_to_all | solution.py:14
  219.7 1.3 collective-permute-start
  291.5 40.0 %copy-start.3 = (f32[1,1024,1024]{2,1,0:T(8,128)S(1)}, f32[1,1024,1024]{2,1,0:T(8,128)}, u32[]{:S(2)}) copy-start(f32[1,1024,1024]{2,1,0:T(8,128)} %param.2) | copy-start | bytes 12582916
  392.5 16.9 %all-to-all-start.14 = ((f32[16,64,256]{2,1,0:T(8,128)}), f32[16,64,256]{2,1,0:T(8,128)S(1)}, u32[]{:S(2)}, u32[]{:S(2)}) async-start(f32[16,64,256]{2,1,0:T(8,128)} %bitcast.24), calls=%async_computation.14 | async-start | bytes 2097152 | tf_op jit(solution)/shard_map/all_to_all | solution.py:14
  409.4 1.7 copy-start
  411.1 20.1 %all-to-all-start.16 = ((f32[4,512,256]{1,2,0:T(8,128)}), f32[4,512,256]{1,2,0:T(8,128)S(1)}, u32[]{:S(2)}, u32[]{:S(2)}) async-start(f32[4,512,256]{1,2,0:T(8,128)} %broadcast_in_dim.47), calls=%async_computation.16 | async-start | bytes 4194304 | tf_op jit(solution)/shard_map/all_to_all | solution.py:14
  450.1 20.1 %all-to-all-start.15 = ((f32[4,512,256]{2,1,0:T(8,128)}), f32[4,512,256]{2,1,0:T(8,128)S(1)}, u32[]{:S(2)}, u32[]{:S(2)}) async-start(f32[4,512,256]{2,1,0:T(8,128)} %broadcast_in_dim.46), calls=%async_computation.15 | async-start | bytes 4194304 | tf_op jit(solution)/shard_map/all_to_all | solution.py:14
  455.0 1.3 collective-permute-start.1
